TPU v7x, 256 devices: a whole 4x4x8 slice. The times are simulated.
256 devices in a mesh: slab: 8 (over z_lo, core), corpus: 32 (over x, z_hi, y).
Axes of the slice: x: 4, y: 4, z: 8 (z_hi: 2, z_lo: 4; z = z_hi * 4 + z_lo), core: 2. Of those that a mesh axis runs over, the one named last changes fastest.
Arguments:
- vectors: bfloat16 [524288, 128], P(('slab', 'corpus')), parts along dimension 0, may hold values from -1.796875 to 1.796875
- docs: int32 [524288], P(('slab', 'corpus')), parts along dimension 0, may hold values from 0 to 63
- prior: float32 [524288], P(('slab', 'corpus')), parts along dimension 0, may hold values from 0.5 to 3
Outputs:
- best: float32 [524288], P(('slab', 'corpus')), parts along dimension 0
There are 8 independent parts, one for each index of `slab`. A program takes and returns all parts, laid end to end along the dimension named above; each array names one. Nothing has to cross between parts.
All inputs are finite; a program needn't handle non-finite values.
Results may differ from a plain program's by a relative error of at most 0.0003.
Values may be sent and summed in bfloat16 or wider, within the bound.
A program may use at most 128 MiB of HBM per device.

v0:
```python
import jax
import jax.numpy as jnp
from jax import lax
from jax.sharding import PartitionSpec as P

ROUNDS = 4


NEG = -1e30


def from_behind(value, axis, steps):
    count = lax.axis_size(axis)
    pairs = [(source, (source + steps) % count) for source in range(count)]
    return lax.ppermute(value, axis, pairs)


def one_tile(own, own_tags, other, other_tags):
    count = own.shape[0]
    rows_blk = min(512, count)
    pieces = count // rows_blk
    colmax = jnp.full((other.shape[0],), NEG, jnp.float32)
    row_parts = []
    for piece in range(pieces):
        rows_x = own[piece * rows_blk : (piece + 1) * rows_blk]
        rows_t = own_tags[piece * rows_blk : (piece + 1) * rows_blk]
        scores = lax.dot_general(
            rows_x, other, (((1,), (1,)), ((), ())), preferred_element_type=jnp.float32
        )
        scores = jnp.where(rows_t[:, None] == other_tags[None, :], NEG, scores)
        colmax = jnp.maximum(colmax, jnp.max(scores, axis=0))
        row_parts.append(jnp.max(scores, axis=1))
    return (jnp.concatenate(row_parts, axis=0), colmax)


def per_device(vectors, docs, prior):
    tags = docs.astype(jnp.bfloat16)
    best = prior
    for dist in range(1, ROUNDS + 1):
        behind, behind_tags = from_behind((vectors, tags), "corpus", dist)
        ahead, ahead_tags = from_behind((vectors, tags), "corpus", -dist)
        rows_one, unused_one = one_tile(vectors, tags, behind, behind_tags)
        rows_two, unused_two = one_tile(vectors, tags, ahead, ahead_tags)
        best = jnp.maximum(best, jnp.maximum(rows_one, rows_two))
    return best


def solution(mesh):
    return jax.shard_map(
        per_device,
        mesh=mesh,
        in_specs=(P(("slab", "corpus"), None), P(("slab", "corpus")), P(("slab", "corpus"))),
        out_specs=P(("slab", "corpus")),
        check_vma=False,
    )
```

profile of v0, /device:TPU:24, one launch (start us, length us, event | category | flops | bytes accessed | tf_op | source)
XLA Modules:
  0.0 191.3 jit_solution(5059960833937243889)
XLA Ops:
  0.0 1.9 %collective-permute-start.11 = (bf16[2048,128]{1,0:T(8,128)(2,1)}, bf16[2048,128]{1,0:T(8,128)(2,1)S(1)}, u32[]{:S(2)}, u32[]{:S(2)}) collective-permute-start(bf16[2048,128]{1,0:T(8,128)(2,1)} %param.3), channel_id=1, source_target_pairs={{0,29},{1,30},{2,31},{3,0},{4,1},{5,2},{6,3},{7,4},{8,5},{9,6},{10... | collective-permute-start | bytes 1572872 | tf_op jit(solution)/shard_map/ppermute | solution.py:15
  1.9 0.7 convert_element_type.3
  2.6 5.4 %collective-permute-start.8 = (bf16[2048]{0:T(1024)(128)(2,1)S(1)}, bf16[2048]{0:T(1024)(128)(2,1)S(1)}, u32[]{:S(2)}, u32[]{:S(2)}) collective-permute-start(bf16[2048]{0:T(1024)(128)(2,1)S(1)} %convert_element_type.3), channel_id=1, source_target_pairs={{0,3},{1,4},{2,5},{3,6},{4,7},{5,8},{6,9},{7,10},{8,11},{9,12},{10... | collective-permute-start | bytes 12296 | tf_op jit(solution)/shard_map/ppermute | solution.py:15
  8.1 4.3 %collective-permute-start.6 = (bf16[2048]{0:T(1024)(128)(2,1)S(1)}, bf16[2048]{0:T(1024)(128)(2,1)S(1)}, u32[]{:S(2)}, u32[]{:S(2)}) collective-permute-start(bf16[2048]{0:T(1024)(128)(2,1)S(1)} %convert_element_type.3), channel_id=1, source_target_pairs={{0,30},{1,31},{2,0},{3,1},{4,2},{5,3},{6,4},{7,5},{8,6},{9,7},{10,... | collective-permute-start | bytes 12296 | tf_op jit(solution)/shard_map/ppermute | solution.py:15
  12.3 9.5 %collective-permute-start.10 = (bf16[2048]{0:T(1024)(128)(2,1)S(1)}, bf16[2048]{0:T(1024)(128)(2,1)S(1)}, u32[]{:S(2)}, u32[]{:S(2)}) collective-permute-start(bf16[2048]{0:T(1024)(128)(2,1)S(1)} %convert_element_type.3), channel_id=1, source_target_pairs={{0,29},{1,30},{2,31},{3,0},{4,1},{5,2},{6,3},{7,4},{8,5},{9,6},{10... | collective-permute-start | bytes 12296 | tf_op jit(solution)/shard_map/ppermute | solution.py:15
  21.9 0.0 collective-permute-start.9
  21.9 1.3 collective-permute-done.10
  23.2 15.9 %collective-permute-start.4 = (bf16[2048]{0:T(1024)(128)(2,1)S(1)}, bf16[2048]{0:T(1024)(128)(2,1)S(1)}, u32[]{:S(2)}, u32[]{:S(2)}) collective-permute-start(bf16[2048]{0:T(1024)(128)(2,1)S(1)} %convert_element_type.3), channel_id=1, source_target_pairs={{0,2},{1,3},{2,4},{3,5},{4,6},{5,7},{6,8},{7,9},{8,10},{9,11},{10,... | collective-permute-start | bytes 12296 | tf_op jit(solution)/shard_map/ppermute | solution.py:15
  39.1 0.0 collective-permute-done.11
  39.1 0.0 collective-permute-start.2
  39.1 1.8 select_reduce_fusion.8
  40.9 0.8 select_reduce_fusion.9
  41.7 0.0 collective-permute-done.8
  41.7 11.4 %collective-permute-start.14 = (bf16[2048]{0:T(1024)(128)(2,1)S(1)}, bf16[2048]{0:T(1024)(128)(2,1)S(1)}, u32[]{:S(2)}, u32[]{:S(2)}) collective-permute-start(bf16[2048]{0:T(1024)(128)(2,1)S(1)} %convert_element_type.3), channel_id=1, source_target_pairs={{0,28},{1,29},{2,30},{3,31},{4,0},{5,1},{6,2},{7,3},{8,4},{9,5},{1... | collective-permute-start | bytes 12296 | tf_op jit(solution)/shard_map/ppermute | solution.py:15
  53.1 0.0 collective-permute-done.9
  53.1 8.6 %collective-permute-start.7 = (bf16[2048,128]{1,0:T(8,128)(2,1)S(1)}, bf16[2048,128]{1,0:T(8,128)(2,1)S(1)}, u32[]{:S(2)}, u32[]{:S(2)}) collective-permute-start(bf16[2048,128]{1,0:T(8,128)(2,1)S(1)} %copy-done.1), channel_id=1, source_target_pairs={{0,30},{1,31},{2,0},{3,1},{4,2},{5,3},{6,4},{7,5},{8,6},{9,7},{10,... | collective-permute-start | bytes 1572872 | tf_op jit(solution)/shard_map/ppermute | solution.py:15
  61.7 0.8 select_reduce_fusion.12
  62.5 0.8 select_reduce_fusion.13
  63.3 0.8 select_reduce_fusion.10
  64.1 0.8 select_reduce_fusion.14
  64.9 0.8 select_reduce_fusion.11
  65.7 0.8 select_reduce_fusion.15
  66.5 0.0 collective-permute-done.6
  66.5 3.1 %collective-permute-start.12 = (bf16[2048]{0:T(1024)(128)(2,1)S(1)}, bf16[2048]{0:T(1024)(128)(2,1)S(1)}, u32[]{:S(2)}, u32[]{:S(2)}) collective-permute-start(bf16[2048]{0:T(1024)(128)(2,1)S(1)} %convert_element_type.3), channel_id=1, source_target_pairs={{0,4},{1,5},{2,6},{3,7},{4,8},{5,9},{6,10},{7,11},{8,12},{9,13},{1... | collective-permute-start | bytes 12296 | tf_op jit(solution)/shard_map/ppermute | solution.py:15
  69.6 16.0 %collective-permute-done.7 = bf16[2048,128]{1,0:T(8,128)(2,1)S(1)} collective-permute-done((bf16[2048,128]{1,0:T(8,128)(2,1)S(1)}, bf16[2048,128]{1,0:T(8,128)(2,1)S(1)}, u32[]{:S(2)}, u32[]{:S(2)}) %collective-permute-start.7) | collective-permute-done | bytes 524320 | tf_op jit(solution)/shard_map/ppermute | solution.py:15
  85.6 0.0 collective-permute-start.5
  85.6 0.8 select_reduce_fusion.16
  86.4 0.8 select_reduce_fusion.17
  87.2 0.8 select_reduce_fusion.18
  88.0 0.8 select_reduce_fusion.19
  88.8 0.0 collective-permute-done.4
  88.8 0.1 collective-permute-start
  88.9 19.5 %collective-permute-done.5 = bf16[2048,128]{1,0:T(8,128)(2,1)S(1)} collective-permute-done((bf16[2048,128]{1,0:T(8,128)(2,1)S(1)}, bf16[2048,128]{1,0:T(8,128)(2,1)S(1)}, u32[]{:S(2)}, u32[]{:S(2)}) %collective-permute-start.5) | collective-permute-done | bytes 524320 | tf_op jit(solution)/shard_map/ppermute | solution.py:15
  108.4 0.0 collective-permute-start.3
  108.4 0.8 select_reduce_fusion.20
  109.2 0.8 select_reduce_fusion.21
  110.0 0.8 select_reduce_fusion.22
  110.9 0.8 select_reduce_fusion.23
  111.7 0.0 collective-permute-done.2
  111.7 8.1 %collective-permute-start.1 = (bf16[2048,128]{1,0:T(8,128)(2,1)S(1)}, bf16[2048,128]{1,0:T(8,128)(2,1)S(1)}, u32[]{:S(2)}, u32[]{:S(2)}) collective-permute-start(bf16[2048,128]{1,0:T(8,128)(2,1)S(1)} %copy-done.1), channel_id=1, source_target_pairs={{0,1},{1,2},{2,3},{3,4},{4,5},{5,6},{6,7},{7,8},{8,9},{9,10},{10,1... | collective-permute-start | bytes 1572872 | tf_op jit(solution)/shard_map/ppermute | solution.py:15
  119.8 7.8 %collective-permute-done.3 = bf16[2048,128]{1,0:T(8,128)(2,1)S(1)} collective-permute-done((bf16[2048,128]{1,0:T(8,128)(2,1)S(1)}, bf16[2048,128]{1,0:T(8,128)(2,1)S(1)}, u32[]{:S(2)}, u32[]{:S(2)}) %collective-permute-start.3) | collective-permute-done | bytes 524320 | tf_op jit(solution)/shard_map/ppermute | solution.py:15
  127.6 7.4 %collective-permute-start.15 = (bf16[2048,128]{1,0:T(8,128)(2,1)S(1)}, bf16[2048,128]{1,0:T(8,128)(2,1)S(1)}, u32[]{:S(2)}, u32[]{:S(2)}) collective-permute-start(bf16[2048,128]{1,0:T(8,128)(2,1)S(1)} %copy-done.1), channel_id=1, source_target_pairs={{0,28},{1,29},{2,30},{3,31},{4,0},{5,1},{6,2},{7,3},{8,4},{9,5},{1... | collective-permute-start | bytes 1572872 | tf_op jit(solution)/shard_map/ppermute | solution.py:15
  135.1 0.8 select_reduce_fusion.24
  135.9 0.8 select_reduce_fusion.25
  136.7 0.8 select_reduce_fusion.26
  137.5 0.8 select_reduce_fusion.27
  138.3 0.0 collective-permute-done
  138.3 0.3 collective-permute-start.13
  138.6 3.1 %collective-permute-done.1 = bf16[2048,128]{1,0:T(8,128)(2,1)S(1)} collective-permute-done((bf16[2048,128]{1,0:T(8,128)(2,1)S(1)}, bf16[2048,128]{1,0:T(8,128)(2,1)S(1)}, u32[]{:S(2)}, u32[]{:S(2)}) %collective-permute-start.1) | collective-permute-done | bytes 524320 | tf_op jit(solution)/shard_map/ppermute | solution.py:15
  141.7 0.8 select_reduce_fusion.28
  142.6 0.8 select_reduce_fusion.29
  143.4 0.8 select_reduce_fusion.30
  144.2 0.8 select_reduce_fusion.31
  145.0 8.0 %collective-permute-done.15 = bf16[2048,128]{1,0:T(8,128)(2,1)S(1)} collective-permute-done((bf16[2048,128]{1,0:T(8,128)(2,1)S(1)}, bf16[2048,128]{1,0:T(8,128)(2,1)S(1)}, u32[]{:S(2)}, u32[]{:S(2)}) %collective-permute-start.15) | collective-permute-done | bytes 524320 | tf_op jit(solution)/shard_map/ppermute | solution.py:15
  153.0 0.8 select_reduce_fusion
  153.8 0.8 select_reduce_fusion.1
  154.6 0.8 select_reduce_fusion.2
  155.4 0.8 select_reduce_fusion.3
  156.2 31.2 %collective-permute-done.13 = bf16[2048,128]{1,0:T(8,128)(2,1)S(1)} collective-permute-done((bf16[2048,128]{1,0:T(8,128)(2,1)S(1)}, bf16[2048,128]{1,0:T(8,128)(2,1)S(1)}, u32[]{:S(2)}, u32[]{:S(2)}) %collective-permute-start.13) | collective-permute-done | bytes 524320 | tf_op jit(solution)/shard_map/ppermute | solution.py:15
  187.4 0.8 select_reduce_fusion.4
  188.2 0.8 select_reduce_fusion.5
  189.0 0.8 select_reduce_fusion.6
  189.9 0.8 select_reduce_fusion.7
  190.7 0.7 fusion.131
  (7 shorter events, 0.0 us)
Async XLA Ops:
  0.0 39.1 %collective-permute-start.11 = (bf16[2048,128]{1,0:T(8,128)(2,1)}, bf16[2048,128]{1,0:T(8,128)(2,1)S(1)}, u32[]{:S(2)}, u32[]{:S(2)}) collective-permute-start(bf16[2048,128]{1,0:T(8,128)(2,1)} %param.3), channel_id=1, source_target_pairs={{0,29},{1,30},{2,31},{3,0},{4,1},{5,2},{6,3},{7,4},{8,5},{9,6},{10... | collective-permute-start | bytes 1572872 | tf_op jit(solution)/shard_map/ppermute | solution.py:15
  2.6 39.0 %collective-permute-start.8 = (bf16[2048]{0:T(1024)(128)(2,1)S(1)}, bf16[2048]{0:T(1024)(128)(2,1)S(1)}, u32[]{:S(2)}, u32[]{:S(2)}) collective-permute-start(bf16[2048]{0:T(1024)(128)(2,1)S(1)} %convert_element_type.3), channel_id=1, source_target_pairs={{0,3},{1,4},{2,5},{3,6},{4,7},{5,8},{6,9},{7,10},{8,11},{9,12},{10... | collective-permute-start | bytes 12296 | tf_op jit(solution)/shard_map/ppermute | solution.py:15
  8.1 58.4 %collective-permute-start.6 = (bf16[2048]{0:T(1024)(128)(2,1)S(1)}, bf16[2048]{0:T(1024)(128)(2,1)S(1)}, u32[]{:S(2)}, u32[]{:S(2)}) collective-permute-start(bf16[2048]{0:T(1024)(128)(2,1)S(1)} %convert_element_type.3), channel_id=1, source_target_pairs={{0,30},{1,31},{2,0},{3,1},{4,2},{5,3},{6,4},{7,5},{8,6},{9,7},{10,... | collective-permute-start | bytes 12296 | tf_op jit(solution)/shard_map/ppermute | solution.py:15
  12.3 10.9 %collective-permute-start.10 = (bf16[2048]{0:T(1024)(128)(2,1)S(1)}, bf16[2048]{0:T(1024)(128)(2,1)S(1)}, u32[]{:S(2)}, u32[]{:S(2)}) collective-permute-start(bf16[2048]{0:T(1024)(128)(2,1)S(1)} %convert_element_type.3), channel_id=1, source_target_pairs={{0,29},{1,30},{2,31},{3,0},{4,1},{5,2},{6,3},{7,4},{8,5},{9,6},{10... | collective-permute-start | bytes 12296 | tf_op jit(solution)/shard_map/ppermute | solution.py:15
  21.9 31.2 %collective-permute-start.9 = (bf16[2048,128]{1,0:T(8,128)(2,1)}, bf16[2048,128]{1,0:T(8,128)(2,1)S(1)}, u32[]{:S(2)}, u32[]{:S(2)}) collective-permute-start(bf16[2048,128]{1,0:T(8,128)(2,1)} %param.3), channel_id=1, source_target_pairs={{0,3},{1,4},{2,5},{3,6},{4,7},{5,8},{6,9},{7,10},{8,11},{9,12},{10... | collective-permute-start | bytes 1572872 | tf_op jit(solution)/shard_map/ppermute | solution.py:15
  23.2 65.6 %collective-permute-start.4 = (bf16[2048]{0:T(1024)(128)(2,1)S(1)}, bf16[2048]{0:T(1024)(128)(2,1)S(1)}, u32[]{:S(2)}, u32[]{:S(2)}) collective-permute-start(bf16[2048]{0:T(1024)(128)(2,1)S(1)} %convert_element_type.3), channel_id=1, source_target_pairs={{0,2},{1,3},{2,4},{3,5},{4,6},{5,7},{6,8},{7,9},{8,10},{9,11},{10,... | collective-permute-start | bytes 12296 | tf_op jit(solution)/shard_map/ppermute | solution.py:15
  39.1 72.6 %collective-permute-start.2 = (bf16[2048]{0:T(1024)(128)(2,1)S(1)}, bf16[2048]{0:T(1024)(128)(2,1)S(1)}, u32[]{:S(2)}, u32[]{:S(2)}) collective-permute-start(bf16[2048]{0:T(1024)(128)(2,1)S(1)} %convert_element_type.3), channel_id=1, source_target_pairs={{0,31},{1,0},{2,1},{3,2},{4,3},{5,4},{6,5},{7,6},{8,7},{9,8},{10,9... | collective-permute-start | bytes 12296 | tf_op jit(solution)/shard_map/ppermute | solution.py:15
  39.1 1.8 copy-start.1
  41.7 103.3 %collective-permute-start.14 = (bf16[2048]{0:T(1024)(128)(2,1)S(1)}, bf16[2048]{0:T(1024)(128)(2,1)S(1)}, u32[]{:S(2)}, u32[]{:S(2)}) collective-permute-start(bf16[2048]{0:T(1024)(128)(2,1)S(1)} %convert_element_type.3), channel_id=1, source_target_pairs={{0,28},{1,29},{2,30},{3,31},{4,0},{5,1},{6,2},{7,3},{8,4},{9,5},{1... | collective-permute-start | bytes 12296 | tf_op jit(solution)/shard_map/ppermute | solution.py:15
  53.1 32.5 %collective-permute-start.7 = (bf16[2048,128]{1,0:T(8,128)(2,1)S(1)}, bf16[2048,128]{1,0:T(8,128)(2,1)S(1)}, u32[]{:S(2)}, u32[]{:S(2)}) collective-permute-start(bf16[2048,128]{1,0:T(8,128)(2,1)S(1)} %copy-done.1), channel_id=1, source_target_pairs={{0,30},{1,31},{2,0},{3,1},{4,2},{5,3},{6,4},{7,5},{8,6},{9,7},{10,... | collective-permute-start | bytes 1572872 | tf_op jit(solution)/shard_map/ppermute | solution.py:15
  66.5 89.7 %collective-permute-start.12 = (bf16[2048]{0:T(1024)(128)(2,1)S(1)}, bf16[2048]{0:T(1024)(128)(2,1)S(1)}, u32[]{:S(2)}, u32[]{:S(2)}) collective-permute-start(bf16[2048]{0:T(1024)(128)(2,1)S(1)} %convert_element_type.3), channel_id=1, source_target_pairs={{0,4},{1,5},{2,6},{3,7},{4,8},{5,9},{6,10},{7,11},{8,12},{9,13},{1... | collective-permute-start | bytes 12296 | tf_op jit(solution)/shard_map/ppermute | solution.py:15
  85.6 22.9 %collective-permute-start.5 = (bf16[2048,128]{1,0:T(8,128)(2,1)S(1)}, bf16[2048,128]{1,0:T(8,128)(2,1)S(1)}, u32[]{:S(2)}, u32[]{:S(2)}) collective-permute-start(bf16[2048,128]{1,0:T(8,128)(2,1)S(1)} %copy-done.1), channel_id=1, source_target_pairs={{0,2},{1,3},{2,4},{3,5},{4,6},{5,7},{6,8},{7,9},{8,10},{9,11},{10,... | collective-permute-start | bytes 1572872 | tf_op jit(solution)/shard_map/ppermute | solution.py:15
  88.8 49.5 %collective-permute-start = (bf16[2048]{0:T(1024)(128)(2,1)S(1)}, bf16[2048]{0:T(1024)(128)(2,1)S(1)}, u32[]{:S(2)}, u32[]{:S(2)}) collective-permute-start(bf16[2048]{0:T(1024)(128)(2,1)S(1)} %convert_element_type.3), channel_id=1, source_target_pairs={{0,1},{1,2},{2,3},{3,4},{4,5},{5,6},{6,7},{7,8},{8,9},{9,10},{10,1... | collective-permute-start | bytes 12296 | tf_op jit(solution)/shard_map/ppermute | solution.py:15
  108.4 19.2 %collective-permute-start.3 = (bf16[2048,128]{1,0:T(8,128)(2,1)S(1)}, bf16[2048,128]{1,0:T(8,128)(2,1)S(1)}, u32[]{:S(2)}, u32[]{:S(2)}) collective-permute-start(bf16[2048,128]{1,0:T(8,128)(2,1)S(1)} %copy-done.1), channel_id=1, source_target_pairs={{0,31},{1,0},{2,1},{3,2},{4,3},{5,4},{6,5},{7,6},{8,7},{9,8},{10,9... | collective-permute-start | bytes 1572872 | tf_op jit(solution)/shard_map/ppermute | solution.py:15
  111.7 30.1 %collective-permute-start.1 = (bf16[2048,128]{1,0:T(8,128)(2,1)S(1)}, bf16[2048,128]{1,0:T(8,128)(2,1)S(1)}, u32[]{:S(2)}, u32[]{:S(2)}) collective-permute-start(bf16[2048,128]{1,0:T(8,128)(2,1)S(1)} %copy-done.1), channel_id=1, source_target_pairs={{0,1},{1,2},{2,3},{3,4},{4,5},{5,6},{6,7},{7,8},{8,9},{9,10},{10,1... | collective-permute-start | bytes 1572872 | tf_op jit(solution)/shard_map/ppermute | solution.py:15
  127.6 25.4 %collective-permute-start.15 = (bf16[2048,128]{1,0:T(8,128)(2,1)S(1)}, bf16[2048,128]{1,0:T(8,128)(2,1)S(1)}, u32[]{:S(2)}, u32[]{:S(2)}) collective-permute-start(bf16[2048,128]{1,0:T(8,128)(2,1)S(1)} %copy-done.1), channel_id=1, source_target_pairs={{0,28},{1,29},{2,30},{3,31},{4,0},{5,1},{6,2},{7,3},{8,4},{9,5},{1... | collective-permute-start | bytes 1572872 | tf_op jit(solution)/shard_map/ppermute | solution.py:15
  138.3 49.1 %collective-permute-start.13 = (bf16[2048,128]{1,0:T(8,128)(2,1)S(1)}, bf16[2048,128]{1,0:T(8,128)(2,1)S(1)}, u32[]{:S(2)}, u32[]{:S(2)}) collective-permute-start(bf16[2048,128]{1,0:T(8,128)(2,1)S(1)} %copy-done.1), channel_id=1, source_target_pairs={{0,4},{1,5},{2,6},{3,7},{4,8},{5,9},{6,10},{7,11},{8,12},{9,13},{1... | collective-permute-start | bytes 1572872 | tf_op jit(solution)/shard_map/ppermute | solution.py:15
  189.8 0.8 copy-start
where the time goes:
time: 191 us
  waiting for transfers between devices  87 us (46%)
  starting transfers between devices  76.1 us (40%)
  matrix products  26.7 us (14%)
    ppermute x16, waiting for transfers between devices, from_behind(): return lax.ppermute(value, axis, pairs)  87 us
    ppermute x16, starting transfers between devices, from_behind(): return lax.ppermute(value, axis, pairs)  76.1 us
    dot_general x32, matrix products, one_tile(): lax.dot_general(rows_x, other, (((1,), (1,)), ((), ())), preferred_elemen...  26.7 us
  transfers between devices with their start and end apart: 16, of which 7 were waited for; matrix products, arithmetic and copies ran while one was open for 13% of the time, Pallas kernels for 0%

commit v1 on v0

v1 whole, which is shorter than its diff:
```python
import functools

import jax
import jax.numpy as jnp
from jax import lax
from jax.experimental import pallas as pl
from jax.experimental.pallas import tpu as pltpu
from jax.sharding import PartitionSpec as P

MESH = pl.DeviceIdType.MESH
NEG = -1e30
TOK = 2048
DIM = 128
LANES = 128
TAG_ROWS = TOK // LANES
Z_PIECES = 8
Z_ROWS = TOK // Z_PIECES
Y_PIECES = 4
Y_ROWS = TOK // Y_PIECES
BODY = 512
FIRST, SECOND = 4, 5


def kernel(
    v_ref, d_ref, o_ref,
    blocks, tags, wide, rows, cols, res, ret,
    own_sem, a_send, a_recv, b_send, b_recv, c_send, c_recv, d_send, d_recv,
    ta_send, ta_recv, tb_send, tb_recv, tc_send, tc_recv, td_send, td_recv,
    z_send, z_recv, r_send, r_recv, tz_send, tz_recv, tr_send, tr_recv,
    m_send, m_recv,
):
    slab, corpus = lax.axis_index("slab"), lax.axis_index("corpus")
    x, zh, y = corpus // 8, (corpus // 4) % 2, corpus % 4
    core = slab % 2
    takes = (zh + core) % 2 == 1
    gives = (zh + core) % 2 == 0

    def place(px, pz, py):
        return (slab, ((px + 4) % 4) * 8 + pz * 4 + (py + 4) % 4)

    other = 1 - zh
    dx = 1 - 2 * zh
    odx = 1 - 2 * other
    mates = [place(x, zh, y + k) for k in (1, 2, 3)]
    recv_greets = mates + [place(x + 1, zh, y), place(x - 1, zh, y), place(x, other, y), place(x - dx, other, y)]
    send_greets = mates + [place(x, other, y), place(x + odx, other, y)]
    barrier = pltpu.get_barrier_semaphore()

    def hello(ids):
        for to in ids:
            pl.semaphore_signal(barrier, inc=1, device_id=to, device_id_type=MESH)
        pl.semaphore_wait(barrier, len(ids))

    up, two, down = (y + 1) % 4, (y + 2) % 4, (y + 3) % 4

    def remote(src, dst, send, recv, to):
        return pltpu.make_async_remote_copy(
            src_ref=src, dst_ref=dst, send_sem=send, recv_sem=recv, device_id=to, device_id_type=MESH
        )

    def span(k, n):
        return pl.ds(k * n, n)

    def a_copy(c):
        return remote(v_ref.at[span(c, Y_ROWS)], blocks.at[y, span(c, Y_ROWS)], a_send.at[c], a_recv.at[c], mates[2])

    def c_copy(c):
        return remote(
            blocks.at[up, span(c, Y_ROWS)], blocks.at[up, span(c, Y_ROWS)], c_send.at[c], c_recv.at[c], mates[2]
        )

    def z_copy(j):
        return remote(
            v_ref.at[span(j, Z_ROWS)], blocks.at[FIRST, span(j, Z_ROWS)], z_send.at[j], z_recv.at[j], place(x, other, y)
        )

    def r_copy(j):
        return remote(
            blocks.at[FIRST, span(j, Z_ROWS)], blocks.at[SECOND, span(j, Z_ROWS)], r_send.at[j], r_recv.at[j],
            place(x + dx, zh, y),
        )

    b_copy = remote(v_ref, blocks.at[y], b_send, b_recv, mates[0])
    d_copy = remote(v_ref, blocks.at[y], d_send, d_recv, mates[1])
    ta_copy = remote(d_ref, tags.at[y], ta_send, ta_recv, mates[2])
    tb_copy = remote(d_ref, tags.at[y], tb_send, tb_recv, mates[0])
    tc_copy = remote(tags.at[up], tags.at[up], tc_send, tc_recv, mates[2])
    td_copy = remote(d_ref, tags.at[y], td_send, td_recv, mates[1])
    tz_copy = remote(d_ref, tags.at[FIRST], tz_send, tz_recv, place(x, other, y))
    tr_copy = remote(tags.at[FIRST], tags.at[SECOND], tr_send, tr_recv, place(x + dx, zh, y))
    own_v = pltpu.make_async_copy(v_ref, blocks.at[y], own_sem.at[0])
    own_d = pltpu.make_async_copy(d_ref, tags.at[y], own_sem.at[1])

    def widen(b):
        eye = lax.broadcasted_iota(jnp.int32, (LANES, LANES), 0) == lax.broadcasted_iota(jnp.int32, (LANES, LANES), 1)
        ones = jnp.ones((LANES, LANES), jnp.bfloat16)
        labels = tags[b].astype(jnp.float32)
        for q in range(TAG_ROWS):
            line = jnp.broadcast_to(labels[q : q + 1, :], (LANES, LANES))
            spread = jnp.where(eye, line, 0.0).astype(jnp.bfloat16)
            wide[b, q * LANES : (q + 1) * LANES, :] = jnp.dot(spread, ones, preferred_element_type=jnp.float32)

    def tile(left, start, right):
        spot = pl.ds(pl.multiple_of(start, BODY), BODY)
        scores = lax.dot_general(
            blocks[left, spot, :], blocks[right], (((1,), (1,)), ((), ())), preferred_element_type=jnp.float32
        )
        marks = wide[left, spot, :]
        labels = tags[right].astype(jnp.float32)
        best = rows[left, spot, :]
        for q in range(TAG_ROWS):
            part = scores[:, q * LANES : (q + 1) * LANES]
            part = jnp.where(marks == labels[q : q + 1, :], NEG, part)
            best = jnp.maximum(best, part)
            peak = jnp.max(part.reshape(BODY // 8, 8, LANES), axis=0)
            cols[right, :, q * LANES : (q + 1) * LANES] = jnp.maximum(
                cols[right, :, q * LANES : (q + 1) * LANES], peak
            )
        rows[left, spot, :] = best

    def tiles(left, start, count, right):
        @pl.loop(0, count)
        def _(k):
            tile(left, start + k * BODY, right)

    def settle(b, from_rows, from_cols):
        for q in range(TAG_ROWS):
            part = slice(q * LANES, (q + 1) * LANES)
            best = jnp.full((1, LANES), NEG, jnp.float32)
            if from_rows:
                best = jnp.max(rows[b, part, :].T, axis=0, keepdims=True)
            if from_cols:
                best = jnp.maximum(best, jnp.max(cols[b, :, part], axis=0, keepdims=True))
            res[b, q : q + 1, :] = best

    def clear():
        @pl.loop(0, 6)
        def _(b):
            rows[b] = jnp.full((TOK, LANES), NEG, jnp.float32)

        @pl.loop(0, 4)
        def _(b):
            cols[b] = jnp.full((8, TOK), NEG, jnp.float32)

    late = jnp.where(y < 2, two, y)
    early = jnp.where(y < 2, y, two)
    late_start = jnp.where(y < 2, 0, TOK // 2)

    def message(b, slot, sem, to):
        return remote(res.at[b], ret.at[slot], m_send.at[sem], m_recv.at[slot], to)

    @pl.when(takes)
    def _():
        own_v.start()
        own_d.start()
        hello(recv_greets)
        ta_copy.start()
        for c in range(Y_PIECES):
            a_copy(c).start()
        tb_copy.start()
        b_copy.start()
        clear()
        own_v.wait()
        own_d.wait()
        widen(y)

        def on_a(c):
            if c == 0:
                ta_copy.wait_recv()
                tc_copy.start()
                widen(up)
            a_copy(c).wait_recv()
            c_copy(c).start()
            tile(up, c * Y_ROWS, y)

        def on_z(j):
            if j == 0:
                tz_copy.wait_recv()
                tr_copy.start()
                widen(FIRST)
            z_copy(j).wait_recv()
            r_copy(j).start()
            if j % 2 == 1:
                tile(FIRST, (j // 2) * BODY, y)

        on_a(0)
        on_a(1)
        on_z(0)
        on_a(2)
        on_z(1)
        on_a(3)
        for j in range(2, Z_PIECES):
            on_z(j)
        tr_copy.wait_recv()
        widen(SECOND)
        for j in range(Z_PIECES):
            r_copy(j).wait_recv()
        tiles(SECOND, 0, TOK // BODY, y)
        minus = jnp.where(zh == 1, FIRST, SECOND)
        plus = jnp.where(zh == 1, SECOND, FIRST)
        tiles(jnp.where(up > y, plus, minus), 0, TOK // BODY, up)
        tc_copy.wait_recv()
        for c in range(Y_PIECES):
            c_copy(c).wait_recv()
        tiles(jnp.where(two > y, plus, minus), 0, TOK // BODY, two)
        tb_copy.wait_recv()
        b_copy.wait_recv()
        tiles(jnp.where(down > y, plus, minus), 0, TOK // BODY, down)
        settle(FIRST, True, False)
        message(FIRST, 0, 3, place(x, other, y)).start()
        settle(SECOND, True, False)
        message(SECOND, 1, 4, place(x - dx, other, y)).start()
        settle(down, False, True)
        message(down, 0, 0, mates[2]).start()
        settle(up, True, True)
        message(up, 2, 1, mates[0]).start()
        widen(two)
        tiles(late, late_start, TOK // 2 // BODY, early)
        settle(two, True, True)
        message(two, 1, 2, mates[1]).start()
        settle(y, True, True)
        for slot in range(3):
            message(y, slot, slot, mates[slot]).wait_recv()
        best = res[y]
        for slot in range(3):
            best = jnp.maximum(best, ret[slot])
        o_ref[...] = best
        ta_copy.wait_send()
        tb_copy.wait_send()
        tc_copy.wait_send()
        tr_copy.wait_send()
        b_copy.wait_send()
        for c in range(Y_PIECES):
            a_copy(c).wait_send()
            c_copy(c).wait_send()
        for j in range(Z_PIECES):
            r_copy(j).wait_send()
        for sem in range(5):
            message(y, 0, sem, mates[0]).wait_send()

    @pl.when(gives)
    def _():
        own_v.start()
        own_d.start()
        hello(send_greets)
        tz_copy.start()
        for j in range(Z_PIECES):
            z_copy(j).start()
        tb_copy.start()
        b_copy.start()
        td_copy.start()
        d_copy.start()
        clear()
        own_v.wait()
        own_d.wait()
        widen(y)
        tb_copy.wait_recv()
        widen(down)
        b_copy.wait_recv()
        tiles(down, 0, TOK // BODY, y)
        settle(down, True, False)
        message(down, 2, 0, mates[2]).start()
        td_copy.wait_recv()
        widen(two)
        d_copy.wait_recv()
        tiles(late, late_start, TOK // 2 // BODY, early)
        settle(two, True, True)
        message(two, 3, 1, mates[1]).start()
        settle(y, True, True)
        best = res[y]
        for slot in (2, 3, 0, 1):
            message(y, slot, 0, mates[0]).wait_recv()
            best = jnp.maximum(best, ret[slot])
        o_ref[...] = best
        tz_copy.wait_send()
        tb_copy.wait_send()
        td_copy.wait_send()
        b_copy.wait_send()
        d_copy.wait_send()
        for j in range(Z_PIECES):
            z_copy(j).wait_send()
        for sem in range(2):
            message(y, 0, sem, mates[0]).wait_send()


def per_device(vectors, docs, prior):
    dma = pltpu.SemaphoreType.DMA
    pair = [dma, dma]
    found = pl.pallas_call(
        kernel,
        out_shape=jax.ShapeDtypeStruct((TAG_ROWS, LANES), jnp.float32),
        in_specs=[pl.BlockSpec(memory_space=pl.ANY)] * 2,
        out_specs=pl.BlockSpec(memory_space=pltpu.VMEM),
        scratch_shapes=[
            pltpu.VMEM((6, TOK, DIM), jnp.bfloat16),
            pltpu.VMEM((6, TAG_ROWS, LANES), jnp.int32),
            pltpu.VMEM((6, TOK, LANES), jnp.float32),
            pltpu.VMEM((6, TOK, LANES), jnp.float32),
            pltpu.VMEM((4, 8, TOK), jnp.float32),
            pltpu.VMEM((6, TAG_ROWS, LANES), jnp.float32),
            pltpu.VMEM((4, TAG_ROWS, LANES), jnp.float32),
            dma((2,)),
            dma((Y_PIECES,)), dma((Y_PIECES,)),
            dma, dma,
            dma((Y_PIECES,)), dma((Y_PIECES,)),
            dma, dma,
            *pair, *pair, *pair, *pair,
            dma((Z_PIECES,)), dma((Z_PIECES,)),
            dma((Z_PIECES,)), dma((Z_PIECES,)),
            *pair, *pair,
            dma((5,)), dma((4,)),
        ],
        compiler_params=pltpu.CompilerParams(collective_id=0, has_side_effects=True),
        name="window",
    )(vectors, docs.reshape(TAG_ROWS, LANES))
    return jnp.maximum(prior, found.reshape(TOK))


def solution(mesh):
    return jax.shard_map(
        per_device,
        mesh=mesh,
        in_specs=(P(("slab", "corpus"), None), P(("slab", "corpus")), P(("slab", "corpus"))),
        out_specs=P(("slab", "corpus")),
        check_vma=False,
    )
```

time: 191 us -> 50.9 us (0.27)
  the two profiles are of different devices: /device:TPU:24 before, /device:TPU:1 now
where the time goes in v1:
time: 50.9 us; the launch traced here: 50.8 us
  Pallas kernels  49.4 us (97%)
  other arithmetic  1.3 us (3%)
    pallas_call x1, Pallas kernels, per_device(): pl.pallas_call(kernel, out_shape=jax.ShapeDtypeStruct((TAG_ROWS, LANES),...  49.4 us
    max x1, other arithmetic, per_device(): return jnp.maximum(prior, found.reshape(TOK))  1.3 us

profile of v1, /device:TPU:1, one launch (start us, length us, event | category | flops | bytes accessed | tf_op | source)
XLA Modules:
  0.0 50.8 jit_solution(5399322063594203109)
XLA Ops:
  0.0 0.0 copy-start
  0.0 49.4 %window.1 = f32[16,128]{1,0:T(8,128)} custom-call(bf16[2048,128]{1,0:T(8,128)(2,1)} %v_ref.1, s32[16,128]{1,0:T(8,128)} %bitcast.3), custom_call_target="tpu_custom_call" | custom-call | tf_op jit(solution)/shard_map/window/pallas_call | solution.py:289
  49.5 0.0 copy-done
  49.5 1.3 %bitcast_maximum_fusion = f32[2048]{0:T(1024)} fusion(f32[2048]{0:T(1024)S(1)} %copy-done, f32[16,128]{1,0:T(8,128)} %window.1), kind=kLoop, calls=%fused_computation | loop fusion | flops 2048 | bytes 24576 | tf_op jit(solution)/shard_map/max | solution.py:316
Async XLA Ops:
  0.0 49.5 %copy-start = (f32[2048]{0:T(1024)S(1)}, f32[2048]{0:T(1024)}, u32[]{:S(2)}) copy-start(f32[2048]{0:T(1024)} %param.5) | copy-start | bytes 24580

commit v2 on v0

v2 whole, which is shorter than its diff:
```python
import jax
import jax.numpy as jnp
from jax import lax
from jax.experimental import pallas as pl
from jax.experimental.pallas import tpu as pltpu
from jax.sharding import PartitionSpec as P

MESH = pl.DeviceIdType.MESH
NEG = -1e30
TOK = 2048
HALF = TOK // 2
DIM = 128
LANES = 128
TAG_ROWS = TOK // LANES
HALF_TAGS = TAG_ROWS // 2
Z_PIECES = 4
Z_ROWS = HALF // Z_PIECES
Y_PIECES = 4
B_AFTER = 1
Y_ROWS = TOK // Y_PIECES
BODY = 512
WIDTH = 512
DIRECT, RELAYED, GROUP = 0, HALF, TOK
BLOCK_ROWS = TOK + 8 * TOK
LEFT_ROWS = TOK + 4 * TOK


def scope(name):
    return jax.named_scope(name)


def kernel(
    v_ref, d_ref, o_ref,
    buf, tags, wide, rows, cols, res, ret,
    own_sem, a_send, a_recv, c_send, c_recv, b_send, b_recv, f_send, f_recv, z_send, z_recv, r_send, r_recv,
    t_send, t_recv, m_send, m_recv,
):
    slab, corpus = lax.axis_index("slab"), lax.axis_index("corpus")
    x, zh, y = corpus // 8, (corpus // 4) % 2, corpus % 4
    core = slab % 2
    takes = (zh + core) % 2 == 1
    gives = (zh + core) % 2 == 0
    half = (zh + core + 1) % 2
    partner = slab + 1 - 2 * core
    other = 1 - zh
    dx = 1 - 2 * zh

    def place(px, pz, py, s=slab):
        return (s, ((px + 4) % 4) * 8 + pz * 4 + (py + 4) % 4)

    def block(b):
        return pl.multiple_of(GROUP + b * TOK, TOK)

    def remote(src, dst, send, recv, to):
        return pltpu.make_async_remote_copy(
            src_ref=src, dst_ref=dst, send_sem=send, recv_sem=recv, device_id=to, device_id_type=MESH
        )

    def at(start, count):
        return buf.at[pl.ds(pl.multiple_of(start, 16), count)]

    def tag_at(start, count):
        return tags.at[pl.ds(pl.multiple_of(start, 8), count)]

    def tag_row(row):
        return row // LANES

    up, two, down = (y + 1) % 4, (y + 2) % 4, (y + 3) % 4
    near = jnp.where(takes, up, down)
    ahead = place(x, zh, jnp.where(takes, y - 1, y + 1))
    group = jnp.where(takes, 0, 4)
    own_row, near_row, two_row = block(y), block(near), block(two)

    barrier = pltpu.get_barrier_semaphore()

    def hello(ids):
        for to in ids:
            pl.semaphore_signal(barrier, inc=1, device_id=to, device_id_type=MESH)
        pl.semaphore_wait(barrier, len(ids))

    mates = [place(x, zh, y + k) for k in (1, 2, 3)]
    cross = [place(x, zh, y + k, partner) for k in (0, 1, 2, 3)]
    sides = [place(x + 1, zh, y), place(x - 1, zh, y)]
    far = [place(x, other, y), place(x - dx, other, y)]
    far_partner = [place(x, other, y, partner), place(x - dx, other, y, partner)]

    def a_copy(c):
        return remote(
            v_ref.at[pl.ds(c * Y_ROWS, Y_ROWS)], at(own_row + c * Y_ROWS, Y_ROWS), a_send.at[c], a_recv.at[c], ahead
        )

    def c_copy(c):
        spot = at(near_row + c * Y_ROWS, Y_ROWS)
        return remote(spot, spot, c_send.at[c], c_recv.at[c], ahead)

    b_copy = remote(v_ref, at(own_row, TOK), b_send, b_recv, mates[0])

    def z_copy(h, j):
        return remote(
            v_ref.at[pl.ds(h * HALF + j * Z_ROWS, Z_ROWS)], at(DIRECT + j * Z_ROWS, Z_ROWS),
            z_send.at[h * Z_PIECES + j], z_recv.at[j], (far if h == 0 else far_partner)[0],
        )

    def r_copy(j):
        return remote(
            at(DIRECT + j * Z_ROWS, Z_ROWS), at(RELAYED + j * Z_ROWS, Z_ROWS), r_send.at[j], r_recv.at[j],
            place(x + dx, zh, y),
        )

    def forward(k):
        src = v_ref if k == 0 else at(block((y + k) % 4), TOK)
        return remote(src, at(block(4 + (y + k) % 4), TOK), f_send.at[k], f_recv.at[k], cross[0])

    def tag_copy(k):
        own_tags, near_tags = tag_row(own_row), tag_row(near_row)
        src, dst, to = [
            (d_ref, tag_at(own_tags, TAG_ROWS), ahead),
            (tag_at(near_tags, TAG_ROWS), tag_at(near_tags, TAG_ROWS), ahead),
            (d_ref, tag_at(own_tags, TAG_ROWS), mates[0]),
            (d_ref.at[pl.ds(0, HALF_TAGS)], tag_at(0, HALF_TAGS), far[0]),
            (d_ref.at[pl.ds(HALF_TAGS, HALF_TAGS)], tag_at(0, HALF_TAGS), far_partner[0]),
            (tag_at(0, HALF_TAGS), tag_at(HALF_TAGS, HALF_TAGS), place(x + dx, zh, y)),
        ][k]
        return remote(src, dst, t_send.at[k], t_recv.at[min(k, 3) if k < 5 else 4], to)

    def tag_forward(k):
        src = d_ref if k == 0 else tag_at(tag_row(block((y + k) % 4)), TAG_ROWS)
        return remote(src, tag_at(tag_row(block(4 + (y + k) % 4)), TAG_ROWS), t_send.at[6 + k], t_recv.at[5 + k], cross[0])

    own_v = pltpu.make_async_copy(v_ref, at(own_row, TOK), own_sem.at[0])
    own_d = pltpu.make_async_copy(d_ref, tag_at(tag_row(own_row), TAG_ROWS), own_sem.at[1])

    def widen(row, count):
        shape = (LANES, LANES)
        eye = lax.broadcasted_iota(jnp.int32, shape, 0) == lax.broadcasted_iota(jnp.int32, shape, 1)
        labels = tags[pl.ds(pl.multiple_of(tag_row(row), 8), count // LANES), :].astype(jnp.float32)
        spread = jnp.concatenate(
            [
                jnp.where(eye, jnp.broadcast_to(labels[q : q + 1, :], shape), 0.0).astype(jnp.bfloat16)
                for q in range(count // LANES)
            ],
            axis=0,
        )
        wide[pl.ds(pl.multiple_of(row, LANES), count), :] = jnp.dot(
            spread, jnp.ones(shape, jnp.bfloat16), preferred_element_type=jnp.float32
        )

    def tile(left, right, first, body=BODY):
        spot = pl.ds(pl.multiple_of(left, BODY), body)
        labels = tags[pl.ds(pl.multiple_of(tag_row(right), 8), TAG_ROWS), :].astype(jnp.float32)
        b = (right - GROUP) // TOK
        for w in range(TOK // WIDTH):
            scores = lax.dot_general(
                buf[spot, :], buf[pl.ds(pl.multiple_of(right + w * WIDTH, WIDTH), WIDTH), :],
                (((1,), (1,)), ((), ())), preferred_element_type=jnp.float32,
            )
            marks = wide[spot, :]
            best = None if first and w == 0 else rows[spot, :]
            for k in range(WIDTH // LANES):
                q = w * (WIDTH // LANES) + k
                part = jnp.where(marks == labels[q : q + 1, :], NEG, scores[:, k * LANES : (k + 1) * LANES])
                best = part if best is None else jnp.maximum(best, part)
                peak = jnp.max(part.reshape(body // 8, 8, LANES), axis=0)
                lanes = slice(q * LANES, (q + 1) * LANES)
                cols[b, :, lanes] = jnp.maximum(cols[b, :, lanes], peak)
            rows[spot, :] = best

    def row_peaks(row, count):
        part = rows[pl.ds(pl.multiple_of(row, LANES), count), :]
        return jnp.max(part.reshape(count // LANES, LANES, LANES), axis=2)

    def col_peaks(b):
        return jnp.concatenate(
            [jnp.max(cols[b, :, q * LANES : (q + 1) * LANES], axis=0, keepdims=True) for q in range(TAG_ROWS)], axis=0
        )

    def message(src, count, dst, send, recv, to):
        slot, start = dst
        return remote(
            res.at[pl.ds(pl.multiple_of(src, 8), count)], ret.at[slot, pl.ds(start, count)],
            m_send.at[send], m_recv.at[recv], to,
        )

    def res_row(b):
        return pl.multiple_of(tag_row(block(b)), TAG_ROWS)

    late = jnp.where(y < 2, two, y)
    early = jnp.where(y < 2, y, two)
    late_row = block(late) + jnp.where(y < 2, 0, HALF)
    minus = jnp.where(zh == 1, DIRECT, RELAYED)
    plus = jnp.where(zh == 1, RELAYED, DIRECT)
    center = block(group + y)

    own_v.start()
    own_d.start()

    with scope("hello"):
        @pl.when(takes)
        def _():
            hello(mates + cross + sides + far)
            tag_forward(0).start()
            forward(0).start()
            tag_copy(0).start()
            for c in range(Y_PIECES):
                a_copy(c).start()

        @pl.when(gives)
        def _():
            hello(mates + cross + sides + far + far_partner)
            tag_copy(3).start()
            tag_copy(4).start()
            for j in range(Z_PIECES):
                z_copy(0, j).start()
                z_copy(1, j).start()
            tag_copy(0).start()
            for c in range(Y_PIECES):
                a_copy(c).start()

    with scope("init"):
        cols[...] = jnp.full(cols.shape, NEG, jnp.float32)
        res[...] = jnp.full(res.shape, NEG, jnp.float32)
        own_v.wait()
        own_d.wait()
        widen(own_row, TOK)

    def pass_on(c, do):
        if c < Y_PIECES // 2:
            getattr(c_copy(c), do)()
        else:
            whole = takes | ((y >= 2) if do == "wait_recv" else (y == 1) | (y == 2))

            @pl.when(whole)
            def _():
                getattr(c_copy(c), do)()

    def on_near(c):
        with scope("near%d" % c):
            if c == 0:
                tag_copy(0).wait_recv()
                tag_copy(1).start()
                widen(near_row, TOK)
            a_copy(c).wait_recv()

            @pl.when(takes)
            def _():
                c_copy(c).start()

            if c == B_AFTER:
                @pl.when(takes)
                def _():
                    tag_copy(2).start()
                    b_copy.start()

            if c == Y_PIECES - 1:
                @pl.when(takes)
                def _():
                    tag_forward(1).start()
                    forward(1).start()

                @pl.when(gives)
                def _():
                    for k in range(Y_PIECES):
                        pass_on(k, "start")
            tile(near_row + c * Y_ROWS, own_row, True)

    def on_z(j):
        with scope("z%d" % j):
            if j == 0:
                tag_copy(3).wait_recv()
                tag_copy(5).start()
            z_copy(0, j).wait_recv()
            r_copy(j).start()

    def on_direct(i):
        with scope("dir%d" % i):
            if i == 0:
                @pl.when(gives)
                def _():
                    tag_forward(0).wait_recv()
                    forward(0).wait_recv()
                widen(DIRECT, HALF)
            tile(DIRECT + i * BODY, center, True)

    def on_two():
        with scope("two"):
            @pl.when(takes)
            def _():
                tag_copy(1).wait_recv()
                for c in range(Y_PIECES):
                    c_copy(c).wait_recv()
                tag_forward(2).start()
                forward(2).start()

    def on_down():
        with scope("down"):
            @pl.when(takes)
            def _():
                tag_copy(2).wait_recv()
                b_copy.wait_recv()
                tag_forward(3).start()
                forward(3).start()

    def others(i, ks):
        for k in ks:
            if i == 0:
                @pl.when(gives)
                def _():
                    tag_forward(k).wait_recv()
                    forward(k).wait_recv()

            b = (y + k) % 4
            tile(jnp.where(b > y, plus, minus) + i * BODY, block(group + b), False)

    def on_relayed(i):
        if i == 0:
            tag_copy(5).wait_recv()
            widen(RELAYED, HALF)
        r_copy(2 * i).wait_recv()
        r_copy(2 * i + 1).wait_recv()
        tile(RELAYED + i * BODY, center, True)

    on_near(0)
    on_near(1)
    on_z(0)
    on_near(2)
    on_z(1)
    on_near(3)
    on_direct(0)
    on_z(2)
    with scope("rel0"):
        on_relayed(0)
    with scope("oth0a"):
        others(0, (1,))
    on_two()
    on_z(3)
    with scope("oth0b"):
        others(0, (2,))
    on_direct(1)
    on_down()
    with scope("oth0c"):
        others(0, (3,))
    with scope("rel1"):
        on_relayed(1)
    with scope("oth1"):
        others(1, (1, 2, 3))

    with scope("zpeaks"):
        res[0:TAG_ROWS, :] = row_peaks(0, TOK)

        @pl.when(takes)
        def _():
            message(0, HALF_TAGS, (0, 0), 0, 0, far[0]).start()
            message(HALF_TAGS, HALF_TAGS, (1, 0), 1, 2, far[1]).start()

        @pl.when(gives)
        def _():
            message(0, HALF_TAGS, (0, HALF_TAGS), 0, 1, far_partner[0]).start()
            message(HALF_TAGS, HALF_TAGS, (1, HALF_TAGS), 1, 3, far_partner[1]).start()
            for k in (1, 2, 3, 0):
                b = 4 + (y + k) % 4
                slot = 3 + (4 - k) % 4
                res[pl.ds(res_row(b), TAG_ROWS), :] = col_peaks(b)
                message(res_row(b), TAG_ROWS, (slot, 0), 4 + k, slot, cross[k]).start()

    with scope("opp"):
        @pl.when(gives)
        def _():
            tag_copy(1).wait_recv()
            for c in range(Y_PIECES):
                pass_on(c, "wait_recv")

        widen(two_row, TOK)
        tile(late_row, block(early), True)
        tile(late_row + BODY, block(early), True)

    with scope("peaks"):
        res[pl.ds(res_row(near), TAG_ROWS), :] = row_peaks(near_row, TOK)
        res[pl.ds(pl.multiple_of(tag_row(late_row), HALF_TAGS), HALF_TAGS), :] = row_peaks(late_row, HALF)
        for k in (2, 1, 3, 0):
            b = (y + k) % 4
            spot = pl.ds(res_row(b), TAG_ROWS)
            res[spot, :] = jnp.maximum(res[spot, :], col_peaks(b))

            @pl.when(takes)
            def _():
                if k:
                    message(res_row(b), TAG_ROWS, (3 - k, 0), 1 + k, 3 - k, mates[k - 1]).start()

            @pl.when(gives)
            def _():
                if k == 3:
                    message(res_row(b), TAG_ROWS, (2, 0), 2, 4, mates[2]).start()
                if k == 2:
                    message(res_row(b), TAG_ROWS, (3, 0), 3, 5, mates[1]).start()

    with scope("final"):
        @pl.when(takes)
        def _():
            best = res[pl.ds(res_row(y), TAG_ROWS), :]
            for slot in range(7):
                message(0, TAG_ROWS, (slot, 0), 0, slot, mates[0]).wait_recv()
                best = jnp.maximum(best, ret[slot])
            o_ref[...] = best

        @pl.when(gives)
        def _():
            best = res[pl.ds(res_row(y), TAG_ROWS), :]
            for slot in (2, 3):
                message(0, TAG_ROWS, (slot, 0), 0, slot + 2, mates[0]).wait_recv()
                best = jnp.maximum(best, ret[slot])
            for sem in range(4):
                message(0, HALF_TAGS, (0, 0), 0, sem, mates[0]).wait_recv()
            for slot in (0, 1):
                best = jnp.maximum(best, ret[slot])
            o_ref[...] = best

    with scope("drain"):
        for c in range(Y_PIECES):
            a_copy(c).wait_send()
            pass_on(c, "wait_send")
        for j in range(Z_PIECES):
            r_copy(j).wait_send()
        for k in (0, 1, 5):
            tag_copy(k).wait_send()

        @pl.when(takes)
        def _():
            b_copy.wait_send()
            tag_copy(2).wait_send()
            for k in range(4):
                forward(k).wait_send()
                tag_forward(k).wait_send()
            for sem in range(5):
                message(0, HALF_TAGS if sem < 2 else TAG_ROWS, (0, 0), sem, 0, mates[0]).wait_send()

        @pl.when(gives)
        def _():
            for j in range(Z_PIECES):
                z_copy(0, j).wait_send()
                z_copy(1, j).wait_send()
            tag_copy(3).wait_send()
            tag_copy(4).wait_send()
            for sem in range(8):
                message(0, HALF_TAGS if sem < 2 else TAG_ROWS, (0, 0), sem, 0, mates[0]).wait_send()


def per_device(vectors, docs, prior):
    dma = pltpu.SemaphoreType.DMA
    found = pl.pallas_call(
        kernel,
        out_shape=jax.ShapeDtypeStruct((TAG_ROWS, LANES), jnp.float32),
        in_specs=[pl.BlockSpec(memory_space=pl.ANY)] * 2,
        out_specs=pl.BlockSpec(memory_space=pltpu.VMEM),
        scratch_shapes=[
            pltpu.VMEM((BLOCK_ROWS, DIM), jnp.bfloat16),
            pltpu.VMEM((BLOCK_ROWS // LANES, LANES), jnp.int32),
            pltpu.VMEM((LEFT_ROWS, LANES), jnp.float32),
            pltpu.VMEM((LEFT_ROWS, LANES), jnp.float32),
            pltpu.VMEM((8, 8, TOK), jnp.float32),
            pltpu.VMEM((BLOCK_ROWS // LANES, LANES), jnp.float32),
            pltpu.VMEM((7, TAG_ROWS, LANES), jnp.float32),
            dma((2,)),
            dma((Y_PIECES,)), dma((Y_PIECES,)),
            dma((Y_PIECES,)), dma((Y_PIECES,)),
            dma, dma,
            dma((4,)), dma((4,)),
            dma((2 * Z_PIECES,)), dma((Z_PIECES,)),
            dma((Z_PIECES,)), dma((Z_PIECES,)),
            dma((10,)), dma((9,)),
            dma((8,)), dma((7,)),
        ],
        compiler_params=pltpu.CompilerParams(collective_id=0, has_side_effects=True),
        name="window",
    )(vectors, docs.reshape(TAG_ROWS, LANES))
    return jnp.maximum(prior, found.reshape(TOK))


def solution(mesh):
    return jax.shard_map(
        per_device,
        mesh=mesh,
        in_specs=(P(("slab", "corpus"), None), P(("slab", "corpus")), P(("slab", "corpus"))),
        out_specs=P(("slab", "corpus")),
        check_vma=False,
    )
```

time: 191 us -> 41.5 us (0.22)
  the two profiles are of different devices: /device:TPU:24 before, /device:TPU:32 now
where the time goes in v2:
time: 41.5 us; the launch traced here: 41.4 us
  Pallas kernels  40.1 us (97%)
  other arithmetic  1.3 us (3%)
    pallas_call x1, Pallas kernels, per_device(): pl.pallas_call(kernel, out_shape=jax.ShapeDtypeStruct((TAG_ROWS, LANES),...  40.1 us
    max x1, other arithmetic, per_device(): return jnp.maximum(prior, found.reshape(TOK))  1.3 us

profile of v2, /device:TPU:32, one launch (start us, length us, event | category | flops | bytes accessed | tf_op | source)
XLA Modules:
  0.0 41.4 jit_solution(3699478465802026990)
XLA Ops:
  0.0 0.0 copy-start
  0.0 40.1 %window.1 = f32[16,128]{1,0:T(8,128)} custom-call(bf16[2048,128]{1,0:T(8,128)(2,1)} %v_ref.1, s32[16,128]{1,0:T(8,128)} %bitcast.3), custom_call_target="tpu_custom_call" | custom-call | tf_op jit(solution)/shard_map/window/pallas_call | solution.py:449
  40.1 0.0 copy-done
  40.1 1.3 %bitcast_maximum_fusion = f32[2048]{0:T(1024)} fusion(f32[2048]{0:T(1024)S(1)} %copy-done, f32[16,128]{1,0:T(8,128)} %window.1), kind=kLoop, calls=%fused_computation | loop fusion | flops 2048 | bytes 24576 | tf_op jit(solution)/shard_map/max | solution.py:475
Async XLA Ops:
  0.0 40.1 %copy-start = (f32[2048]{0:T(1024)S(1)}, f32[2048]{0:T(1024)}, u32[]{:S(2)}) copy-start(f32[2048]{0:T(1024)} %param.5) | copy-start | bytes 24580

commit v3 on v2

--- a/solution.py
+++ b/solution.py
@@ -16,9 +16,9 @@
 Z_PIECES = 4
 Z_ROWS = HALF // Z_PIECES
 Y_PIECES = 4
-B_AFTER = 1
 Y_ROWS = TOK // Y_PIECES
 BODY = 512
+GROUPS = ((0, 512), (512, 256), (768, 256))
 WIDTH = 512
 DIRECT, RELAYED, GROUP = 0, HALF, TOK
 BLOCK_ROWS = TOK + 8 * TOK
@@ -73,14 +73,14 @@
 
     barrier = pltpu.get_barrier_semaphore()
 
-    def hello(ids):
-        for to in ids:
+    def hello(greeted, awaited):
+        for to in greeted:
             pl.semaphore_signal(barrier, inc=1, device_id=to, device_id_type=MESH)
-        pl.semaphore_wait(barrier, len(ids))
+        pl.semaphore_wait(barrier, awaited)
 
     mates = [place(x, zh, y + k) for k in (1, 2, 3)]
     cross = [place(x, zh, y + k, partner) for k in (0, 1, 2, 3)]
-    sides = [place(x + 1, zh, y), place(x - 1, zh, y)]
+    feeder = place(x - dx, zh, y)
     far = [place(x, other, y), place(x - dx, other, y)]
     far_partner = [place(x, other, y, partner), place(x - dx, other, y, partner)]
 
@@ -93,7 +93,11 @@
         spot = at(near_row + c * Y_ROWS, Y_ROWS)
         return remote(spot, spot, c_send.at[c], c_recv.at[c], ahead)
 
-    b_copy = remote(v_ref, at(own_row, TOK), b_send, b_recv, mates[0])
+    def b_copy(c):
+        return remote(
+            v_ref.at[pl.ds(c * Y_ROWS, Y_ROWS)], at(own_row + c * Y_ROWS, Y_ROWS), b_send.at[c], b_recv.at[c], mates[0]
+        )
+
 
     def z_copy(h, j):
         return remote(
@@ -146,7 +150,7 @@
         )
 
     def tile(left, right, first, body=BODY):
-        spot = pl.ds(pl.multiple_of(left, BODY), body)
+        spot = pl.ds(pl.multiple_of(left, body), body)
         labels = tags[pl.ds(pl.multiple_of(tag_row(right), 8), TAG_ROWS), :].astype(jnp.float32)
         b = (right - GROUP) // TOK
         for w in range(TOK // WIDTH):
@@ -191,22 +195,32 @@
     plus = jnp.where(zh == 1, RELAYED, DIRECT)
     center = block(group + y)
 
+    def start_b(c):
+        if c == 0:
+            tag_copy(2).start()
+        b_copy(c).start()
+
     own_v.start()
     own_d.start()
 
     with scope("hello"):
         @pl.when(takes)
         def _():
-            hello(mates + cross + sides + far)
-            tag_forward(0).start()
-            forward(0).start()
+            hello([far[0], feeder, *mates, *cross], 5)
             tag_copy(0).start()
             for c in range(Y_PIECES):
                 a_copy(c).start()
+            tag_forward(0).start()
+            forward(0).start()
+
+            @pl.when(zh == 0)
+            def _():
+                for c in range(Y_PIECES):
+                    start_b(c)
 
         @pl.when(gives)
         def _():
-            hello(mates + cross + sides + far + far_partner)
+            hello([far_partner[0], feeder, *mates, cross[0]], 10)
             tag_copy(3).start()
             tag_copy(4).start()
             for j in range(Z_PIECES):
@@ -237,31 +251,22 @@
         with scope("near%d" % c):
             if c == 0:
                 tag_copy(0).wait_recv()
-                tag_copy(1).start()
                 widen(near_row, TOK)
             a_copy(c).wait_recv()
-
-            @pl.when(takes)
-            def _():
-                c_copy(c).start()
-
-            if c == B_AFTER:
-                @pl.when(takes)
-                def _():
-                    tag_copy(2).start()
-                    b_copy.start()
-
-            if c == Y_PIECES - 1:
-                @pl.when(takes)
-                def _():
-                    tag_forward(1).start()
-                    forward(1).start()
-
-                @pl.when(gives)
-                def _():
-                    for k in range(Y_PIECES):
-                        pass_on(k, "start")
             tile(near_row + c * Y_ROWS, own_row, True)
+
+    def on_receiver_near(c):
+        a_copy(c).wait_recv()
+        c_copy(c).start()
+        if c == Y_PIECES - 1:
+            tag_forward(1).start()
+            forward(1).start()
+
+        @pl.when(zh == 1)
+        def _():
+            start_b(c)
+
+        tile(near_row + c * Y_ROWS, own_row, True)
 
     def on_z(j):
         with scope("z%d" % j):
@@ -278,8 +283,10 @@
                 def _():
                     tag_forward(0).wait_recv()
                     forward(0).wait_recv()
-                widen(DIRECT, HALF)
-            tile(DIRECT + i * BODY, center, True)
+                tag_copy(5).wait_recv()
+                widen(DIRECT, TOK)
+            start, count = GROUPS[i]
+            tile(DIRECT + start, center, True, count)
 
     def on_two():
         with scope("two"):
@@ -296,11 +303,13 @@
             @pl.when(takes)
             def _():
                 tag_copy(2).wait_recv()
-                b_copy.wait_recv()
+                for c in range(Y_PIECES):
+                    b_copy(c).wait_recv()
                 tag_forward(3).start()
                 forward(3).start()
 
     def others(i, ks):
+        start, count = GROUPS[i]
         for k in ks:
             if i == 0:
                 @pl.when(gives)
@@ -309,40 +318,80 @@
                     forward(k).wait_recv()
 
             b = (y + k) % 4
-            tile(jnp.where(b > y, plus, minus) + i * BODY, block(group + b), False)
+            tile(jnp.where(b > y, plus, minus) + start, block(group + b), False, count)
 
     def on_relayed(i):
-        if i == 0:
-            tag_copy(5).wait_recv()
-            widen(RELAYED, HALF)
-        r_copy(2 * i).wait_recv()
-        r_copy(2 * i + 1).wait_recv()
-        tile(RELAYED + i * BODY, center, True)
-
-    on_near(0)
-    on_near(1)
+        start, count = GROUPS[i]
+        for j in range(start // Z_ROWS, (start + count) // Z_ROWS):
+            r_copy(j).wait_recv()
+        tile(RELAYED + start, center, True, count)
+
+    @pl.when(takes)
+    def _():
+        with scope("recv01"):
+            tag_copy(0).wait_recv()
+            tag_copy(1).start()
+            widen(near_row, TOK)
+            on_receiver_near(0)
+            on_receiver_near(1)
+
     on_z(0)
-    on_near(2)
+
+    @pl.when(takes)
+    def _():
+        with scope("recv23"):
+            on_receiver_near(2)
+            on_receiver_near(3)
+
+    @pl.when(gives)
+    def _():
+        on_near(0)
+        on_near(1)
+
     on_z(1)
-    on_near(3)
     on_direct(0)
+
+    @pl.when(gives)
+    def _():
+        tag_copy(1).start()
+        pass_on(0, "start")
+        pass_on(1, "start")
+        for c in (2, 3):
+            with scope("near%d" % c):
+                a_copy(c).wait_recv()
+                pass_on(c, "start")
+                tile(near_row + c * Y_ROWS, own_row, True)
+
     on_z(2)
+
+    @pl.when(gives)
+    def _():
+        with scope("adj"):
+            res[pl.ds(res_row(near), TAG_ROWS), :] = row_peaks(near_row, TOK)
+            message(res_row(near), TAG_ROWS, (2, 0), 2, 4, mates[2]).start()
+
+    on_two()
+    on_down()
+    on_direct(1)
     with scope("rel0"):
         on_relayed(0)
     with scope("oth0a"):
         others(0, (1,))
-    on_two()
     on_z(3)
     with scope("oth0b"):
         others(0, (2,))
-    on_direct(1)
-    on_down()
+
     with scope("oth0c"):
         others(0, (3,))
     with scope("rel1"):
         on_relayed(1)
     with scope("oth1"):
         others(1, (1, 2, 3))
+    on_direct(2)
+    with scope("rel2"):
+        on_relayed(2)
+    with scope("oth2"):
+        others(2, (1, 2, 3))
 
     with scope("zpeaks"):
         res[0:TAG_ROWS, :] = row_peaks(0, TOK)
@@ -362,6 +411,21 @@
                 res[pl.ds(res_row(b), TAG_ROWS), :] = col_peaks(b)
                 message(res_row(b), TAG_ROWS, (slot, 0), 4 + k, slot, cross[k]).start()
 
+    def settle(k):
+        spot = pl.ds(res_row((y + k) % 4), TAG_ROWS)
+        res[spot, :] = jnp.maximum(res[spot, :], col_peaks((y + k) % 4))
+
+    def to_mate(k):
+        settle(k)
+        message(res_row((y + k) % 4), TAG_ROWS, (3 - k, 0), 1 + k, 3 - k, mates[k - 1]).start()
+
+    @pl.when(takes)
+    def _():
+        with scope("rpeaks"):
+            res[pl.ds(res_row(near), TAG_ROWS), :] = row_peaks(near_row, TOK)
+            to_mate(1)
+            to_mate(3)
+
     with scope("opp"):
         @pl.when(gives)
         def _():
@@ -374,24 +438,18 @@
         tile(late_row + BODY, block(early), True)
 
     with scope("peaks"):
-        res[pl.ds(res_row(near), TAG_ROWS), :] = row_peaks(near_row, TOK)
         res[pl.ds(pl.multiple_of(tag_row(late_row), HALF_TAGS), HALF_TAGS), :] = row_peaks(late_row, HALF)
-        for k in (2, 1, 3, 0):
-            b = (y + k) % 4
-            spot = pl.ds(res_row(b), TAG_ROWS)
-            res[spot, :] = jnp.maximum(res[spot, :], col_peaks(b))
-
-            @pl.when(takes)
-            def _():
-                if k:
-                    message(res_row(b), TAG_ROWS, (3 - k, 0), 1 + k, 3 - k, mates[k - 1]).start()
-
-            @pl.when(gives)
-            def _():
-                if k == 3:
-                    message(res_row(b), TAG_ROWS, (2, 0), 2, 4, mates[2]).start()
-                if k == 2:
-                    message(res_row(b), TAG_ROWS, (3, 0), 3, 5, mates[1]).start()
+
+        @pl.when(takes)
+        def _():
+            to_mate(2)
+
+        @pl.when(gives)
+        def _():
+            settle(2)
+            message(res_row(two), TAG_ROWS, (3, 0), 3, 5, mates[1]).start()
+
+        settle(0)
 
     with scope("final"):
         @pl.when(takes)
@@ -425,7 +483,8 @@
 
         @pl.when(takes)
         def _():
-            b_copy.wait_send()
+            for c in range(Y_PIECES):
+                b_copy(c).wait_send()
             tag_copy(2).wait_send()
             for k in range(4):
                 forward(k).wait_send()
@@ -448,7 +507,7 @@
     dma = pltpu.SemaphoreType.DMA
     found = pl.pallas_call(
         kernel,
-        out_shape=jax.ShapeDtypeStruct((TAG_ROWS, LANES), jnp.float32),
+        out_shape=pltpu.VMEM((TAG_ROWS, LANES), jnp.float32),
         in_specs=[pl.BlockSpec(memory_space=pl.ANY)] * 2,
         out_specs=pl.BlockSpec(memory_space=pltpu.VMEM),
         scratch_shapes=[
@@ -462,7 +521,7 @@
             dma((2,)),
             dma((Y_PIECES,)), dma((Y_PIECES,)),
             dma((Y_PIECES,)), dma((Y_PIECES,)),
-            dma, dma,
+            dma((Y_PIECES,)), dma((Y_PIECES,)),
             dma((4,)), dma((4,)),
             dma((2 * Z_PIECES,)), dma((Z_PIECES,)),
             dma((Z_PIECES,)), dma((Z_PIECES,)),

time: 41.5 us -> 37.5 us (0.904)
  Pallas kernels: 40.1 us -> 36.8 us
  other arithmetic: 1.3 us -> 0.6 us
    pallas_call x1, Pallas kernels: 40.1 us -> 36.8 us  [per_device(): pl.pallas_call(kernel, out_shape=pltpu.VMEM((TAG_ROWS, LANES), jnp.float3...]
    max x1, other arithmetic: 1.3 us -> 0.6 us  [per_device(): return jnp.maximum(prior, found.reshape(TOK))]
where the time goes in v3:
time: 37.5 us; the launch traced here: 37.4 us
  Pallas kernels  36.8 us (98%)
  other arithmetic  0.6 us (2%)
    pallas_call x1, Pallas kernels, per_device(): pl.pallas_call(kernel, out_shape=pltpu.VMEM((TAG_ROWS, LANES), jnp.float3...  36.8 us

profile of v3, /device:TPU:32, one launch (start us, length us, event | category | flops | bytes accessed | tf_op | source)
XLA Modules:
  0.0 37.4 jit_solution(18440968412832956859)
XLA Ops:
  0.0 0.0 copy-start
  0.0 36.8 %window.1 = f32[16,128]{1,0:T(8,128)S(1)} custom-call(bf16[2048,128]{1,0:T(8,128)(2,1)} %v_ref.1, s32[16,128]{1,0:T(8,128)} %bitcast.3), custom_call_target="tpu_custom_call" | custom-call | tf_op jit(solution)/shard_map/window/pallas_call | solution.py:508
  36.8 0.0 copy-done
  36.8 0.6 %bitcast_maximum_fusion = f32[2048]{0:T(1024)} fusion(f32[2048]{0:T(1024)S(1)} %copy-done, f32[16,128]{1,0:T(8,128)S(1)} %window.1), kind=kLoop, calls=%fused_computation | loop fusion | flops 2048 | bytes 24576 | tf_op jit(solution)/shard_map/max | solution.py:534
Async XLA Ops:
  0.0 36.8 %copy-start = (f32[2048]{0:T(1024)S(1)}, f32[2048]{0:T(1024)}, u32[]{:S(2)}) copy-start(f32[2048]{0:T(1024)} %param.5) | copy-start | bytes 24580

commit v4 on v3

--- a/solution.py
+++ b/solution.py
@@ -13,7 +13,7 @@
 LANES = 128
 TAG_ROWS = TOK // LANES
 HALF_TAGS = TAG_ROWS // 2
-Z_PIECES = 4
+Z_PIECES = 8
 Z_ROWS = HALF // Z_PIECES
 Y_PIECES = 4
 Y_ROWS = TOK // Y_PIECES
@@ -111,9 +111,15 @@
             place(x + dx, zh, y),
         )
 
-    def forward(k):
-        src = v_ref if k == 0 else at(block((y + k) % 4), TOK)
-        return remote(src, at(block(4 + (y + k) % 4), TOK), f_send.at[k], f_recv.at[k], cross[0])
+    def forward(k, h=0):
+        row, their = block((y + k) % 4), block(4 + (y + k) % 4)
+        count = TOK if k < 2 else HALF
+        sem = k if k < 2 else 2 * k - 2 + h
+        src = v_ref if k == 0 else at(row + h * HALF, count)
+        return remote(src, at(their + h * HALF, count), f_send.at[sem], f_recv.at[sem], cross[0])
+
+    def halves(k):
+        return (0,) if k < 2 else (0, 1)
 
     def tag_copy(k):
         own_tags, near_tags = tag_row(own_row), tag_row(near_row)
@@ -150,7 +156,7 @@
         )
 
     def tile(left, right, first, body=BODY):
-        spot = pl.ds(pl.multiple_of(left, body), body)
+        spot = pl.ds(pl.multiple_of(left, LANES), body)
         labels = tags[pl.ds(pl.multiple_of(tag_row(right), 8), TAG_ROWS), :].astype(jnp.float32)
         b = (right - GROUP) // TOK
         for w in range(TOK // WIDTH):
@@ -226,9 +232,10 @@
             for j in range(Z_PIECES):
                 z_copy(0, j).start()
                 z_copy(1, j).start()
-            tag_copy(0).start()
-            for c in range(Y_PIECES):
-                a_copy(c).start()
+                if j == 0:
+                    tag_copy(0).start()
+                if j % 2 == 1:
+                    a_copy(j // 2).start()
 
     with scope("init"):
         cols[...] = jnp.full(cols.shape, NEG, jnp.float32)
@@ -273,8 +280,9 @@
             if j == 0:
                 tag_copy(3).wait_recv()
                 tag_copy(5).start()
-            z_copy(0, j).wait_recv()
-            r_copy(j).start()
+            for piece in (2 * j, 2 * j + 1):
+                z_copy(0, piece).wait_recv()
+                r_copy(piece).start()
 
     def on_direct(i):
         with scope("dir%d" % i):
@@ -288,25 +296,27 @@
             start, count = GROUPS[i]
             tile(DIRECT + start, center, True, count)
 
-    def on_two():
-        with scope("two"):
+    def on_two(h):
+        with scope("two%d" % h):
             @pl.when(takes)
             def _():
-                tag_copy(1).wait_recv()
-                for c in range(Y_PIECES):
+                if h == 0:
+                    tag_copy(1).wait_recv()
+                    tag_forward(2).start()
+                for c in (2 * h, 2 * h + 1):
                     c_copy(c).wait_recv()
-                tag_forward(2).start()
-                forward(2).start()
-
-    def on_down():
-        with scope("down"):
+                forward(2, h).start()
+
+    def on_down(h):
+        with scope("down%d" % h):
             @pl.when(takes)
             def _():
-                tag_copy(2).wait_recv()
-                for c in range(Y_PIECES):
+                if h == 0:
+                    tag_copy(2).wait_recv()
+                    tag_forward(3).start()
+                for c in (2 * h, 2 * h + 1):
                     b_copy(c).wait_recv()
-                tag_forward(3).start()
-                forward(3).start()
+                forward(3, h).start()
 
     def others(i, ks):
         start, count = GROUPS[i]
@@ -315,7 +325,8 @@
                 @pl.when(gives)
                 def _():
                     tag_forward(k).wait_recv()
-                    forward(k).wait_recv()
+                    for h in halves(k):
+                        forward(k, h).wait_recv()
 
             b = (y + k) % 4
             tile(jnp.where(b > y, plus, minus) + start, block(group + b), False, count)
@@ -370,13 +381,15 @@
             res[pl.ds(res_row(near), TAG_ROWS), :] = row_peaks(near_row, TOK)
             message(res_row(near), TAG_ROWS, (2, 0), 2, 4, mates[2]).start()
 
-    on_two()
-    on_down()
+    on_two(0)
     on_direct(1)
     with scope("rel0"):
         on_relayed(0)
+    on_two(1)
+    on_down(0)
     with scope("oth0a"):
         others(0, (1,))
+    on_down(1)
     on_z(3)
     with scope("oth0b"):
         others(0, (2,))
@@ -394,17 +407,25 @@
         others(2, (1, 2, 3))
 
     with scope("zpeaks"):
-        res[0:TAG_ROWS, :] = row_peaks(0, TOK)
+        res[HALF_TAGS:TAG_ROWS, :] = row_peaks(RELAYED, HALF)
 
         @pl.when(takes)
         def _():
+            message(HALF_TAGS, HALF_TAGS, (1, 0), 1, 2, far[1]).start()
+
+        @pl.when(gives)
+        def _():
+            message(HALF_TAGS, HALF_TAGS, (1, HALF_TAGS), 1, 3, far_partner[1]).start()
+
+        res[0:HALF_TAGS, :] = row_peaks(DIRECT, HALF)
+
+        @pl.when(takes)
+        def _():
             message(0, HALF_TAGS, (0, 0), 0, 0, far[0]).start()
-            message(HALF_TAGS, HALF_TAGS, (1, 0), 1, 2, far[1]).start()
 
         @pl.when(gives)
         def _():
             message(0, HALF_TAGS, (0, HALF_TAGS), 0, 1, far_partner[0]).start()
-            message(HALF_TAGS, HALF_TAGS, (1, HALF_TAGS), 1, 3, far_partner[1]).start()
             for k in (1, 2, 3, 0):
                 b = 4 + (y + k) % 4
                 slot = 3 + (4 - k) % 4
@@ -487,7 +508,8 @@
                 b_copy(c).wait_send()
             tag_copy(2).wait_send()
             for k in range(4):
-                forward(k).wait_send()
+                for h in halves(k):
+                    forward(k, h).wait_send()
                 tag_forward(k).wait_send()
             for sem in range(5):
                 message(0, HALF_TAGS if sem < 2 else TAG_ROWS, (0, 0), sem, 0, mates[0]).wait_send()
@@ -522,7 +544,7 @@
             dma((Y_PIECES,)), dma((Y_PIECES,)),
             dma((Y_PIECES,)), dma((Y_PIECES,)),
             dma((Y_PIECES,)), dma((Y_PIECES,)),
-            dma((4,)), dma((4,)),
+            dma((6,)), dma((6,)),
             dma((2 * Z_PIECES,)), dma((Z_PIECES,)),
             dma((Z_PIECES,)), dma((Z_PIECES,)),
             dma((10,)), dma((9,)),

time: 37.5 us -> 37.6 us (level)
  no operation moved by 1% of the time
where the time goes in v4:
time: 37.6 us; the launch traced here: 37.5 us
  Pallas kernels  36.9 us (98%)
  other arithmetic  0.6 us (2%)
    pallas_call x1, Pallas kernels, per_device(): pl.pallas_call(kernel, out_shape=pltpu.VMEM((TAG_ROWS, LANES), jnp.float3...  36.9 us

profile of v4, /device:TPU:32, one launch (start us, length us, event | category | flops | bytes accessed | tf_op | source)
XLA Modules:
  0.0 37.5 jit_solution(14078202588816762705)
XLA Ops:
  0.0 0.0 copy-start
  0.0 36.9 %window.1 = f32[16,128]{1,0:T(8,128)S(1)} custom-call(bf16[2048,128]{1,0:T(8,128)(2,1)} %v_ref.1, s32[16,128]{1,0:T(8,128)} %bitcast.3), custom_call_target="tpu_custom_call" | custom-call | tf_op jit(solution)/shard_map/window/pallas_call | solution.py:530
  36.9 0.0 copy-done
  36.9 0.6 %bitcast_maximum_fusion = f32[2048]{0:T(1024)} fusion(f32[2048]{0:T(1024)S(1)} %copy-done, f32[16,128]{1,0:T(8,128)S(1)} %window.1), kind=kLoop, calls=%fused_computation | loop fusion | flops 2048 | bytes 24576 | tf_op jit(solution)/shard_map/max | solution.py:556
Async XLA Ops:
  0.0 36.9 %copy-start = (f32[2048]{0:T(1024)S(1)}, f32[2048]{0:T(1024)}, u32[]{:S(2)}) copy-start(f32[2048]{0:T(1024)} %param.5) | copy-start | bytes 24580

commit v5 on v4

--- a/solution.py
+++ b/solution.py
@@ -13,7 +13,7 @@
 LANES = 128
 TAG_ROWS = TOK // LANES
 HALF_TAGS = TAG_ROWS // 2
-Z_PIECES = 8
+Z_PIECES = 4
 Z_ROWS = HALF // Z_PIECES
 Y_PIECES = 4
 Y_ROWS = TOK // Y_PIECES
@@ -156,7 +156,7 @@
         )
 
     def tile(left, right, first, body=BODY):
-        spot = pl.ds(pl.multiple_of(left, LANES), body)
+        spot = pl.ds(pl.multiple_of(left, body), body)
         labels = tags[pl.ds(pl.multiple_of(tag_row(right), 8), TAG_ROWS), :].astype(jnp.float32)
         b = (right - GROUP) // TOK
         for w in range(TOK // WIDTH):
@@ -232,10 +232,9 @@
             for j in range(Z_PIECES):
                 z_copy(0, j).start()
                 z_copy(1, j).start()
-                if j == 0:
-                    tag_copy(0).start()
-                if j % 2 == 1:
-                    a_copy(j // 2).start()
+            tag_copy(0).start()
+            for c in range(Y_PIECES):
+                a_copy(c).start()
 
     with scope("init"):
         cols[...] = jnp.full(cols.shape, NEG, jnp.float32)
@@ -280,9 +279,8 @@
             if j == 0:
                 tag_copy(3).wait_recv()
                 tag_copy(5).start()
-            for piece in (2 * j, 2 * j + 1):
-                z_copy(0, piece).wait_recv()
-                r_copy(piece).start()
+            z_copy(0, j).wait_recv()
+            r_copy(j).start()
 
     def on_direct(i):
         with scope("dir%d" % i):

time: 37.6 us -> 37.7 us (level)
  no operation moved by 1% of the time
where the time goes in v5:
time: 37.7 us; the launch traced here: 37.6 us
  Pallas kernels  37 us (98%)
  other arithmetic  0.6 us (2%)
    pallas_call x1, Pallas kernels, per_device(): pl.pallas_call(kernel, out_shape=pltpu.VMEM((TAG_ROWS, LANES), jnp.float3...  37 us

profile of v5, /device:TPU:32, one launch (start us, length us, event | category | flops | bytes accessed | tf_op | source)
XLA Modules:
  0.0 37.6 jit_solution(6747792715092041246)
XLA Ops:
  0.0 0.0 copy-start
  0.0 37.0 %window.1 = f32[16,128]{1,0:T(8,128)S(1)} custom-call(bf16[2048,128]{1,0:T(8,128)(2,1)} %v_ref.1, s32[16,128]{1,0:T(8,128)} %bitcast.3), custom_call_target="tpu_custom_call" | custom-call | tf_op jit(solution)/shard_map/window/pallas_call | solution.py:528
  37.0 0.0 copy-done
  37.0 0.6 %bitcast_maximum_fusion = f32[2048]{0:T(1024)} fusion(f32[2048]{0:T(1024)S(1)} %copy-done, f32[16,128]{1,0:T(8,128)S(1)} %window.1), kind=kLoop, calls=%fused_computation | loop fusion | flops 2048 | bytes 24576 | tf_op jit(solution)/shard_map/max | solution.py:554
Async XLA Ops:
  0.0 37.0 %copy-start = (f32[2048]{0:T(1024)S(1)}, f32[2048]{0:T(1024)}, u32[]{:S(2)}) copy-start(f32[2048]{0:T(1024)} %param.5) | copy-start | bytes 24580
